TPU v7x, 32 devices: a whole 2x2x4 slice. The times are simulated.
32 devices in a mesh: row: 4 (over y, core), col: 8 (over z, x).
Axes of the slice: x: 2, y: 2, z: 4, core: 2. Of those that a mesh axis runs over, the one named last changes fastest.
Arguments:
- inverse: float32 [16384, 16384], P('row', 'col'), may hold values from -6 to 6
- front_blocks: int32 [2, 16], replicated, may hold values from 0 to 63, as said below
- panels: float32 [2, 4096, 256], P(None, 'row'), may hold values from -0.09375 to 0.09375
- diag_terms: float32 [2, 256, 256], replicated, may hold values from -6 to 6
- bounds: int32 [2, 4], replicated, may hold values from 1 to 128, 256 in all within a row
Outputs:
- border: float32 [2, 4096, 256], P(None, ('row', 'col'))
- diag_block: float32 [2, 256, 256], replicated
Inputs may be any that keep to these rules, and one draw needn't show every extreme that they name: `front_blocks`: each row names 16 distinct blocks. Positions 4 r to 4 r + 3 name blocks of four different groups of 16 consecutive blocks, and every such group is named at exactly four positions, of four different r. Positions 2 o and 2 o + 1 name blocks of two different groups of 8 consecutive blocks, and every such group is named at exactly two positions, of two different o.
All inputs are finite; a program needn't handle non-finite values.
Results may differ from a plain program's by a relative error of at most 0.0001.
Values sent between devices are 32-bit elements; how exact they have to be, the bound alone decides.
A program may use at most 128 MiB of HBM per device.

v0:
```python
import jax
import jax.numpy as jnp
from jax import lax
from jax.sharding import PartitionSpec as P

BS = 256


def body(inverse, front_blocks, panels, diag_terms, bounds):
    n_row = lax.axis_size("row")
    n_col = lax.axis_size("col")
    row_index = lax.axis_index("row")
    col_index = lax.axis_index("col")
    rows_loc, cols_loc = inverse.shape
    row_group = rows_loc // BS
    col_group = cols_loc // BS
    list_length = front_blocks.shape[1]
    per_owner = list_length // n_row
    highest = lax.Precision.HIGHEST
    borders = []
    diagonals = []
    for front_index in range(2):
        front_list = front_blocks[front_index]
        own_blocks = lax.dynamic_slice_in_dim(front_list, row_index * per_owner, per_owner)
        w_loc = panels[front_index]
        panel_width = w_loc.shape[1]
        w_pieces = w_loc.reshape(per_owner, BS, panel_width)
        targets = col_index * col_group + jnp.arange(col_group, dtype=jnp.int32)
        picker = (own_blocks[None, :] == targets[:, None]).astype(jnp.float32)
        own_piece = jnp.einsum("ki,iab->ab", picker, w_pieces, precision=highest)
        slot_rows = lax.all_gather(own_piece, "row", axis=0, tiled=True).reshape(
            n_row, BS, panel_width
        )
        owners = front_list.reshape(n_row, per_owner)
        placer = jnp.sum((owners[None, :, :] == targets[:, None, None]).astype(jnp.float32), axis=2)
        w_tilde = jnp.einsum("ks,sab->kab", placer, slot_rows, precision=highest).reshape(
            cols_loc, panel_width
        )
        dest_lists = front_list.reshape(n_row, per_owner)
        local_ids = row_index * row_group + jnp.arange(row_group, dtype=jnp.int32)
        share_rows = per_owner * BS // n_col
        full_rows = jnp.dot(inverse, w_tilde, precision=highest)
        quarters = BS // share_rows
        full_pieces = full_rows.reshape(row_group, quarters, share_rows, panel_width)
        first_rows = jnp.arange(n_col, dtype=jnp.int32) * share_rows
        dest_block = dest_lists[:, first_rows // BS]
        block_pick = (dest_block.T[:, :, None] == local_ids[None, None, :]).astype(jnp.float32)
        quarter_pick = (
            (first_rows % BS // share_rows)[:, None]
            == jnp.arange(quarters, dtype=jnp.int32)[None, :]
        ).astype(jnp.float32)
        sectioned = jnp.einsum("cq,kqap->ckap", quarter_pick, full_pieces, precision=highest)
        ordered = jnp.einsum("cdk,ckap->cdap", block_pick, sectioned, precision=highest)
        ordered = ordered.reshape(n_col * n_row * share_rows, panel_width)
        reduced = lax.psum_scatter(ordered, "col", scatter_dimension=0, tiled=True)
        received = lax.all_to_all(
            reduced.reshape(n_row, share_rows, panel_width),
            "row",
            split_axis=0,
            concat_axis=0,
            tiled=True,
        )
        product = jnp.sum(received, axis=0)
        w_mine = lax.dynamic_slice_in_dim(w_loc, col_index * share_rows, share_rows, 0)
        own_term = jnp.dot(w_mine.T, product, precision=highest)
        summed_total = lax.psum(own_term, ("row", "col"))
        node_ends = jnp.cumsum(bounds[front_index])
        columns = jnp.arange(panel_width, dtype=jnp.int32)
        node_ids = jnp.sum((columns[:, None] >= node_ends[None, :]).astype(jnp.int32), axis=1)
        same_node = (node_ids[:, None] == node_ids[None, :]).astype(jnp.float32)
        borders.append(-product)
        diagonals.append(same_node * (diag_terms[front_index] + summed_total))
    return (jnp.stack(borders), jnp.stack(diagonals))


def solution(mesh):
    placed = (P("row", "col"), P(), P(None, "row", None), P(), P())
    return jax.shard_map(
        body,
        mesh=mesh,
        in_specs=placed,
        out_specs=(P(None, ("row", "col"), None), P()),
        check_vma=False,
    )
```

profile of v0, /device:TPU:0, one launch (start us, length us, event | category | flops | bytes accessed | tf_op | source)
XLA Modules:
  0.0 484.4 jit_solution(6554460476007873666)
XLA Ops:
  7.2 0.8 slice_reduce_fusion.1
  8.0 1.7 fusion.46
  10.0 2.3 fusion.6
  12.3 0.7 copy.51
  13.1 2.3 fusion.4
  15.5 0.7 copy.50
  17.2 15.4 %all-gather.3.cloned.1.call-done = f32[1024,256]{1,0:T(8,128)} async-done(((f32[256,256]{1,0:T(8,128)}), f32[1024,256]{1,0:T(8,128)}) %all-gather.3.cloned.1.call-update) | async-done | bytes 1048592 | tf_op jit(solution)/shard_map/all_gather | solution.py:31
  32.6 4.0 fusion.10
  37.4 58.5 %convolution_bitcast_fusion.1 = f32[4096,256]{0,1:T(8,128)} fusion(f32[2048,256]{1,0:T(8,128)S(1)} %bitcast.104, f32[4096,2048]{1,0:T(8,128)} %param.5), kind=kOutput, calls=%fused_computation.7 | convolution fusion | flops 25769803776 | bytes 39845888 | tf_op jit(solution)/shard_map/dot_general | solution.py:42
  95.9 6.6 %reshape.215 = f32[16,2,128,256]{2,1,0,3:T(2,128)} reshape(f32[4096,256]{0,1:T(8,128)} %convolution_bitcast_fusion.1) | data formatting | bytes 8388608 | tf_op jit(solution)/shard_map/reshape | solution.py:44
  102.5 9.3 %copy.20 = f32[16,2,128,256]{3,1,2,0:T(2,128)} copy(f32[16,2,128,256]{2,1,0,3:T(2,128)} %reshape.215) | data formatting | bytes 8388608 | tf_op jit(solution)/shard_map/reshape | solution.py:44
  111.8 11.7 %fusion.34 = f32[8,16,128,256]{3,0,2,1:T(8,128)S(1)} fusion(f32[16,2,128,256]{3,1,2,0:T(2,128)} %copy.20, s32[8]{0:T(128)S(1)} %and_select_fusion), kind=kOutput, calls=%fused_computation.58 | convolution fusion | flops 100663312 | bytes 20971552 | tf_op jit(solution)/shard_map/cq,kqap->ckap/dot_general | solution.py:52
  123.5 12.2 %fusion.2 = f32[8,4,128,256]{3,1,2,0:T(4,128)S(1)} fusion(f32[8,16,128,256]{3,0,2,1:T(8,128)S(1)} %fusion.34, s32[16]{0:T(128)S(1)} %iota_add_fusion.1, s32[8,4]{1,0:T(8,128)S(1)} %gather_fusion), kind=kOutput, calls=%fused_computation.4 | convolution fusion | flops 201327104 | bytes 20971712 | tf_op jit(solution)/shard_map/cdk,ckap->cdap/dot_general | solution.py:53
  135.7 2.7 copy.22
  139.1 4.0 fusion.8
  143.2 0.7 copy.25
  143.8 58.8 %convolution_bitcast_fusion = f32[4096,256]{0,1:T(8,128)} fusion(f32[2048,256]{1,0:T(8,128)S(1)} %bitcast.105, f32[4096,2048]{1,0:T(8,128)} %param.5), kind=kOutput, calls=%fused_computation.6 | convolution fusion | flops 25769803776 | bytes 39845888 | tf_op jit(solution)/shard_map/dot_general | solution.py:42
  202.6 6.7 %reshape.220 = f32[16,2,128,256]{2,1,0,3:T(2,128)} reshape(f32[4096,256]{0,1:T(8,128)} %convolution_bitcast_fusion) | data formatting | bytes 8388608 | tf_op jit(solution)/shard_map/reshape | solution.py:44
  209.3 9.3 %copy.26 = f32[16,2,128,256]{3,1,2,0:T(2,128)} copy(f32[16,2,128,256]{2,1,0,3:T(2,128)} %reshape.220) | data formatting | bytes 8388608 | tf_op jit(solution)/shard_map/reshape | solution.py:44
  218.6 11.7 %fusion.32 = f32[8,16,128,256]{3,0,2,1:T(8,128)S(1)} fusion(f32[16,2,128,256]{3,1,2,0:T(2,128)} %copy.26, s32[8]{0:T(128)S(1)} %and_select_fusion), kind=kOutput, calls=%fused_computation.56 | convolution fusion | flops 100663312 | bytes 20971552 | tf_op jit(solution)/shard_map/cq,kqap->ckap/dot_general | solution.py:52
  230.3 12.2 %fusion = f32[8,4,128,256]{3,1,2,0:T(4,128)S(1)} fusion(f32[8,16,128,256]{3,0,2,1:T(8,128)S(1)} %fusion.32, s32[8,4]{1,0:T(8,128)S(1)} %gather_fusion.1, s32[16]{0:T(128)S(1)} %iota_add_fusion.1), kind=kOutput, calls=%fused_computation.2 | convolution fusion | flops 201327104 | bytes 20971712 | tf_op jit(solution)/shard_map/cdk,ckap->cdap/dot_general | solution.py:53
  242.5 2.7 copy.28
  245.3 3.6 all-to-all-start
  249.4 84.5 %reduce-scatter.5.cloned.1.call-done = f32[512,256]{1,0:T(8,128)} async-done(((f32[4096,256]{1,0:T(8,128)}), f32[512,256]{1,0:T(8,128)}) %reduce-scatter.5.cloned.1.call-update) | async-done | bytes 524304 | tf_op jit(solution)/shard_map/reduce_scatter | solution.py:55
  333.9 3.5 all-to-all-start.1
  337.5 2.1 fusion.18
  339.5 6.6 %all-to-all-done.1 = f32[4,128,256]{2,1,0:T(8,128)S(1)} async-done(((f32[4,128,256]{2,1,0:T(8,128)}), f32[4,128,256]{2,1,0:T(8,128)S(1)}, u32[]{:S(2)}, u32[]{:S(2)}) %all-to-all-start.1) | async-done | bytes 524320 | tf_op jit(solution)/shard_map/all_to_all | solution.py:56
  346.2 1.1 fusion.16
  347.3 0.7 pad_maximum_fusion.1
  348.1 127.4 %all-reduce.3.cloned.1.call-done = (f32[256,256]{1,0:T(8,128)}, f32[256,256]{1,0:T(8,128)}) async-done(((f32[256,256]{1,0:T(8,128)}, f32[256,256]{1,0:T(8,128)}), (f32[256,256]{1,0:T(8,128)}, f32[256,256]{1,0:T(8,128)})) %all-reduce.3.cloned.1.call-update) | async-done | bytes 524304 | tf_op jit(solution)/shard_map/psum | solution.py:66
  475.5 1.2 fusion.15
  476.7 0.8 pad_maximum_fusion
  (42 shorter events, 3.4 us)
Async XLA Ops:
  7.2 25.5 %all-gather.3.cloned.1.call-start = ((), (), s32[]{:S(2)}) async-start(), calls=%async_computation.4 | async-start | bytes 1310720 | tf_op jit(solution)/shard_map/all_gather | solution.py:31
  9.7 27.7 %copy-start = (f32[1,1024,256]{2,1,0:T(8,128)}, f32[1,1024,256]{2,1,0:T(8,128)S(1)}, u32[]{:S(2)}) copy-start(f32[1,1024,256]{2,1,0:T(8,128)S(1)} %get-tuple-element.10) | copy-start | bytes 3145732
  13.1 126.1 %all-gather.5.cloned.1.call-start = ((), (), s32[]{:S(2)}) async-start(), calls=%async_computation.6 | async-start | bytes 1310720 | tf_op jit(solution)/shard_map/all_gather | solution.py:31
  16.2 229.1 %reduce-scatter.3.cloned.1.call-start = ((), (), s32[]{:S(2)}) async-start(), calls=%async_computation.5 | async-start | bytes 4718592 | tf_op jit(solution)/shard_map/reduce_scatter | solution.py:55
  138.4 195.5 %reduce-scatter.5.cloned.1.call-start = ((), (), s32[]{:S(2)}) async-start(), calls=%async_computation.7 | async-start | bytes 4718592 | tf_op jit(solution)/shard_map/reduce_scatter | solution.py:55
  245.2 3.7 copy-start.2
  245.2 230.3 %copy-start.1 = (f32[2,256,256]{2,1,0:T(8,128)S(1)}, f32[2,256,256]{2,1,0:T(8,128)}, u32[]{:S(2)}) copy-start(f32[2,256,256]{2,1,0:T(8,128)} %param.8) | copy-start | bytes 1572868
  245.3 88.6 %all-to-all-start = ((f32[4,128,256]{2,1,0:T(8,128)}), f32[4,128,256]{2,1,0:T(8,128)S(1)}, u32[]{:S(2)}, u32[]{:S(2)}) async-start(f32[4,128,256]{2,1,0:T(8,128)} %bitcast.112), calls=%async_computation.1 | async-start | bytes 1048576 | tf_op jit(solution)/shard_map/all_to_all | solution.py:56
  333.9 12.3 %all-to-all-start.1 = ((f32[4,128,256]{2,1,0:T(8,128)}), f32[4,128,256]{2,1,0:T(8,128)S(1)}, u32[]{:S(2)}, u32[]{:S(2)}) async-start(f32[4,128,256]{2,1,0:T(8,128)} %bitcast.113), calls=%async_computation.3 | async-start | bytes 1048576 | tf_op jit(solution)/shard_map/all_to_all | solution.py:56
  337.3 138.2 %all-reduce.3.cloned.1.call-start = ((), (), s32[]{:S(2)}) async-start(), calls=%async_computation.8 | async-start | bytes 1048576 | tf_op jit(solution)/shard_map/psum | solution.py:66
Sparse Core Ops, SparseCore 0:
  13.2 19.4 all-gather.2
  34.8 16.6 all-gather.4
  138.5 88.2 reduce-scatter.2
  245.4 88.4 reduce-scatter.4
  347.4 128.0 all-reduce.2
where the time goes:
time: 492 us; the launch traced here: 484 us
  waiting for transfers between devices  234 us (48%)
  matrix products  181 us (37%)
  local copies, waits for them, and re-layouts  44.1 us (9%)
  between operations  14.4 us (3%)
  starting transfers between devices  7.29 us (1%)
    psum x1, waiting for transfers between devices, body(): summed_total = lax.psum(own_term, ('row', 'col'))  127 us
    dot_general x2, matrix products, body(): full_rows = jnp.dot(inverse, w_tilde, precision=highest)  117 us
    reduce_scatter x2, waiting for transfers between devices, body(): reduced = lax.psum_scatter(ordered, 'col', scatter_dimension=0, tiled=True)  84.5 us
    reshape x4, local copies, waits for them, and re-layouts, body(): full_rows.reshape(row_group, quarters, share_rows, panel_width)  31.9 us
    dot_general x2, matrix products, body(): jnp.einsum('cdk,ckap->cdap', block_pick, sectioned, precision=highest)  24.4 us
    dot_general x2, matrix products, body(): jnp.einsum('cq,kqap->ckap', quarter_pick, full_pieces, precision=highest)  23.4 us
    all_gather x2, waiting for transfers between devices, body(): lax.all_gather(own_piece, 'row', axis=0, tiled=True)  15.4 us
  transfers between devices with their start and end apart: 7, of which 4 were waited for; matrix products, arithmetic and copies ran while one was open for 45% of the time, Pallas kernels for 0%

commit v1 on v0

--- a/solution.py
+++ b/solution.py
@@ -63,7 +63,7 @@
         product = jnp.sum(received, axis=0)
         w_mine = lax.dynamic_slice_in_dim(w_loc, col_index * share_rows, share_rows, 0)
         own_term = jnp.dot(w_mine.T, product, precision=highest)
-        summed_total = lax.psum(own_term, ("row", "col"))
+        summed_total = lax.psum(lax.psum(own_term, "row"), "col")
         node_ends = jnp.cumsum(bounds[front_index])
         columns = jnp.arange(panel_width, dtype=jnp.int32)
         node_ids = jnp.sum((columns[:, None] >= node_ends[None, :]).astype(jnp.int32), axis=1)

time: 492 us -> 473 us (0.961)
  waiting for transfers between devices: 234 us -> 214 us
    psum x1 -> x2, waiting for transfers between devices: 127 us -> 107 us  [body(): summed_total = lax.psum(lax.psum(own_term, 'row'), 'col')]
  transfers between devices with their start and end apart: 7 -> 8, of which waited for: 4 -> 5; matrix products, arithmetic and copies ran while one was open for 45% -> 47% of each run, Pallas kernels for 0% -> 0%
where the time goes in v1:
time: 473 us; the launch traced here: 465 us
  waiting for transfers between devices  214 us (45%)
  matrix products  181 us (38%)
  local copies, waits for them, and re-layouts  44.1 us (9%)
  between operations  14.7 us (3%)
  starting transfers between devices  7.33 us (2%)
    dot_general x2, matrix products, body(): full_rows = jnp.dot(inverse, w_tilde, precision=highest)  117 us
    psum x2, waiting for transfers between devices, body(): summed_total = lax.psum(lax.psum(own_term, 'row'), 'col')  107 us
    reduce_scatter x2, waiting for transfers between devices, body(): reduced = lax.psum_scatter(ordered, 'col', scatter_dimension=0, tiled=True)  85 us
    reshape x4, local copies, waits for them, and re-layouts, body(): full_rows.reshape(row_group, quarters, share_rows, panel_width)  31.9 us
    dot_general x2, matrix products, body(): jnp.einsum('cdk,ckap->cdap', block_pick, sectioned, precision=highest)  24.4 us
    dot_general x2, matrix products, body(): jnp.einsum('cq,kqap->ckap', quarter_pick, full_pieces, precision=highest)  23.4 us
    all_gather x2, waiting for transfers between devices, body(): lax.all_gather(own_piece, 'row', axis=0, tiled=True)  15.4 us
  transfers between devices with their start and end apart: 8, of which 5 were waited for; matrix products, arithmetic and copies ran while one was open for 47% of the time, Pallas kernels for 0%

profile of v1, /device:TPU:0, one launch (start us, length us, event | category | flops | bytes accessed | tf_op | source)
XLA Modules:
  0.0 465.2 jit_solution(10666742543191495199)
XLA Ops:
  7.2 0.8 slice_reduce_fusion.1
  8.0 1.7 fusion.46
  10.0 2.3 fusion.6
  12.3 0.7 copy.51
  13.1 2.3 fusion.4
  15.5 0.7 copy.50
  17.2 15.4 %all-gather.3.cloned.1.call-done = f32[1024,256]{1,0:T(8,128)} async-done(((f32[256,256]{1,0:T(8,128)}), f32[1024,256]{1,0:T(8,128)}) %all-gather.3.cloned.1.call-update) | async-done | bytes 1048592 | tf_op jit(solution)/shard_map/all_gather | solution.py:31
  32.6 4.0 fusion.10
  37.4 58.5 %convolution_bitcast_fusion.1 = f32[4096,256]{0,1:T(8,128)} fusion(f32[2048,256]{1,0:T(8,128)S(1)} %bitcast.104, f32[4096,2048]{1,0:T(8,128)} %param.5), kind=kOutput, calls=%fused_computation.7 | convolution fusion | flops 25769803776 | bytes 39845888 | tf_op jit(solution)/shard_map/dot_general | solution.py:42
  95.9 6.6 %reshape.215 = f32[16,2,128,256]{2,1,0,3:T(2,128)} reshape(f32[4096,256]{0,1:T(8,128)} %convolution_bitcast_fusion.1) | data formatting | bytes 8388608 | tf_op jit(solution)/shard_map/reshape | solution.py:44
  102.5 9.3 %copy.20 = f32[16,2,128,256]{3,1,2,0:T(2,128)} copy(f32[16,2,128,256]{2,1,0,3:T(2,128)} %reshape.215) | data formatting | bytes 8388608 | tf_op jit(solution)/shard_map/reshape | solution.py:44
  111.8 11.7 %fusion.34 = f32[8,16,128,256]{3,0,2,1:T(8,128)S(1)} fusion(f32[16,2,128,256]{3,1,2,0:T(2,128)} %copy.20, s32[8]{0:T(128)S(1)} %and_select_fusion), kind=kOutput, calls=%fused_computation.58 | convolution fusion | flops 100663312 | bytes 20971552 | tf_op jit(solution)/shard_map/cq,kqap->ckap/dot_general | solution.py:52
  123.5 12.2 %fusion.2 = f32[8,4,128,256]{3,1,2,0:T(4,128)S(1)} fusion(f32[8,16,128,256]{3,0,2,1:T(8,128)S(1)} %fusion.34, s32[16]{0:T(128)S(1)} %iota_add_fusion.1, s32[8,4]{1,0:T(8,128)S(1)} %gather_fusion), kind=kOutput, calls=%fused_computation.4 | convolution fusion | flops 201327104 | bytes 20971712 | tf_op jit(solution)/shard_map/cdk,ckap->cdap/dot_general | solution.py:53
  135.7 2.7 copy.22
  139.1 4.0 fusion.8
  143.8 58.8 %convolution_bitcast_fusion = f32[4096,256]{0,1:T(8,128)} fusion(f32[2048,256]{1,0:T(8,128)S(1)} %bitcast.105, f32[4096,2048]{1,0:T(8,128)} %param.5), kind=kOutput, calls=%fused_computation.6 | convolution fusion | flops 25769803776 | bytes 39845888 | tf_op jit(solution)/shard_map/dot_general | solution.py:42
  202.6 6.7 %reshape.220 = f32[16,2,128,256]{2,1,0,3:T(2,128)} reshape(f32[4096,256]{0,1:T(8,128)} %convolution_bitcast_fusion) | data formatting | bytes 8388608 | tf_op jit(solution)/shard_map/reshape | solution.py:44
  209.3 9.3 %copy.26 = f32[16,2,128,256]{3,1,2,0:T(2,128)} copy(f32[16,2,128,256]{2,1,0,3:T(2,128)} %reshape.220) | data formatting | bytes 8388608 | tf_op jit(solution)/shard_map/reshape | solution.py:44
  218.6 11.7 %fusion.32 = f32[8,16,128,256]{3,0,2,1:T(8,128)S(1)} fusion(f32[16,2,128,256]{3,1,2,0:T(2,128)} %copy.26, s32[8]{0:T(128)S(1)} %and_select_fusion), kind=kOutput, calls=%fused_computation.56 | convolution fusion | flops 100663312 | bytes 20971552 | tf_op jit(solution)/shard_map/cq,kqap->ckap/dot_general | solution.py:52
  230.3 12.2 %fusion = f32[8,4,128,256]{3,1,2,0:T(4,128)S(1)} fusion(f32[8,16,128,256]{3,0,2,1:T(8,128)S(1)} %fusion.32, s32[8,4]{1,0:T(8,128)S(1)} %gather_fusion.1, s32[16]{0:T(128)S(1)} %iota_add_fusion.1), kind=kOutput, calls=%fused_computation.2 | convolution fusion | flops 201327104 | bytes 20971712 | tf_op jit(solution)/shard_map/cdk,ckap->cdap/dot_general | solution.py:53
  242.5 2.7 copy.28
  245.3 3.6 all-to-all-start
  248.9 84.9 %reduce-scatter.5.cloned.1.call-done = f32[512,256]{1,0:T(8,128)} async-done(((f32[4096,256]{1,0:T(8,128)}), f32[512,256]{1,0:T(8,128)}) %reduce-scatter.5.cloned.1.call-update) | async-done | bytes 524304 | tf_op jit(solution)/shard_map/reduce_scatter | solution.py:55
  333.9 3.5 all-to-all-start.1
  337.4 2.0 fusion.18
  339.5 6.7 %all-to-all-done.1 = f32[4,128,256]{2,1,0:T(8,128)S(1)} async-done(((f32[4,128,256]{2,1,0:T(8,128)}), f32[4,128,256]{2,1,0:T(8,128)S(1)}, u32[]{:S(2)}, u32[]{:S(2)}) %all-to-all-start.1) | async-done | bytes 524320 | tf_op jit(solution)/shard_map/all_to_all | solution.py:56
  346.2 1.1 fusion.16
  347.8 31.9 %all-reduce.7.cloned.1.call-done = (f32[256,256]{1,0:T(8,128)}, f32[256,256]{1,0:T(8,128)}) async-done(((f32[256,256]{1,0:T(8,128)}, f32[256,256]{1,0:T(8,128)}), (f32[256,256]{1,0:T(8,128)}, f32[256,256]{1,0:T(8,128)})) %all-reduce.7.cloned.1.call-update) | async-done | bytes 524304 | tf_op jit(solution)/shard_map/psum | solution.py:66
  379.8 0.7 pad_maximum_fusion.1
  380.5 75.4 %all-reduce.5.cloned.1.call-done = (f32[256,256]{1,0:T(8,128)}, f32[256,256]{1,0:T(8,128)}) async-done(((f32[256,256]{1,0:T(8,128)}, f32[256,256]{1,0:T(8,128)}), (f32[256,256]{1,0:T(8,128)}, f32[256,256]{1,0:T(8,128)})) %all-reduce.5.cloned.1.call-update) | async-done | bytes 524304 | tf_op jit(solution)/shard_map/psum | solution.py:66
  455.9 1.2 fusion.15
  457.1 0.8 pad_maximum_fusion
  (45 shorter events, 4.2 us)
Async XLA Ops:
  7.2 25.5 %all-gather.3.cloned.1.call-start = ((), (), s32[]{:S(2)}) async-start(), calls=%async_computation.4 | async-start | bytes 1310720 | tf_op jit(solution)/shard_map/all_gather | solution.py:31
  9.7 27.7 %copy-start = (f32[1,1024,256]{2,1,0:T(8,128)}, f32[1,1024,256]{2,1,0:T(8,128)S(1)}, u32[]{:S(2)}) copy-start(f32[1,1024,256]{2,1,0:T(8,128)S(1)} %get-tuple-element.12) | copy-start | bytes 3145732
  13.1 126.1 %all-gather.5.cloned.1.call-start = ((), (), s32[]{:S(2)}) async-start(), calls=%async_computation.6 | async-start | bytes 1310720 | tf_op jit(solution)/shard_map/all_gather | solution.py:31
  16.2 229.1 %reduce-scatter.3.cloned.1.call-start = ((), (), s32[]{:S(2)}) async-start(), calls=%async_computation.5 | async-start | bytes 4718592 | tf_op jit(solution)/shard_map/reduce_scatter | solution.py:55
  138.4 195.5 %reduce-scatter.5.cloned.1.call-start = ((), (), s32[]{:S(2)}) async-start(), calls=%async_computation.7 | async-start | bytes 4718592 | tf_op jit(solution)/shard_map/reduce_scatter | solution.py:55
  245.2 102.1 %copy-start.2 = (s32[2,4]{1,0:T(2,128)S(1)}, s32[2,4]{1,0:T(2,128)}, u32[]{:S(2)}) copy-start(s32[2,4]{1,0:T(2,128)} %param.9) | copy-start | bytes 100
  245.3 210.7 %copy-start.1 = (f32[2,256,256]{2,1,0:T(8,128)S(1)}, f32[2,256,256]{2,1,0:T(8,128)}, u32[]{:S(2)}) copy-start(f32[2,256,256]{2,1,0:T(8,128)} %param.8) | copy-start | bytes 1572868
  245.3 88.6 %all-to-all-start = ((f32[4,128,256]{2,1,0:T(8,128)}), f32[4,128,256]{2,1,0:T(8,128)S(1)}, u32[]{:S(2)}, u32[]{:S(2)}) async-start(f32[4,128,256]{2,1,0:T(8,128)} %bitcast.112), calls=%async_computation.1 | async-start | bytes 1048576 | tf_op jit(solution)/shard_map/all_to_all | solution.py:56
  333.9 12.3 %all-to-all-start.1 = ((f32[4,128,256]{2,1,0:T(8,128)}), f32[4,128,256]{2,1,0:T(8,128)S(1)}, u32[]{:S(2)}, u32[]{:S(2)}) async-start(f32[4,128,256]{2,1,0:T(8,128)} %bitcast.113), calls=%async_computation.3 | async-start | bytes 1048576 | tf_op jit(solution)/shard_map/all_to_all | solution.py:56
  337.3 42.4 %all-reduce.7.cloned.1.call-start = ((), (), s32[]{:S(2)}) async-start(), calls=%async_computation.9 | async-start | bytes 1048576 | tf_op jit(solution)/shard_map/psum | solution.py:66
  347.3 108.6 %all-reduce.5.cloned.1.call-start = ((), (), s32[]{:S(2)}) async-start(), calls=%async_computation.8 | async-start | bytes 1048576 | tf_op jit(solution)/shard_map/psum | solution.py:66
Sparse Core Ops, SparseCore 0:
  13.2 19.4 all-gather.2
  34.8 16.6 all-gather.4
  138.5 88.2 reduce-scatter.2
  245.4 88.4 reduce-scatter.4
  347.4 32.2 all-reduce.6
  383.0 72.8 all-reduce.4
